TPU v7x, 128 devices: a whole 4x4x4 slice. The times are simulated.
128 devices in a mesh: lon: 32 (over x_hi, z, y), ch: 4 (over x_lo, core).
Axes of the slice: x: 4 (x_hi: 2, x_lo: 2; x = x_hi * 2 + x_lo), y: 4, z: 4, core: 2. Of those that a mesh axis runs over, the one named last changes fastest.
Arguments:
- ocean_state: bfloat16 [400, 64, 4096], P('ch', None, 'lon'), may hold values from -6 to 6
- sea_mask: int32 [64, 4096], P(None, 'lon'), may hold values 0 or 1
- kernel: float32 [400, 49], P('ch'), may hold values from -0.875 to 0.875
- conv_bias: float32 [400], P('ch'), may hold values from -3 to 3
- norm_gain: float32 [400], replicated, may hold values from 0.1 to 1.9
- norm_bias: float32 [400], replicated, may hold values from -2 to 2
- weight_in: bfloat16 [400, 1600], replicated, may hold values from -0.3125 to 0.3125
- bias_in: float32 [1600], replicated, may hold values from -3 to 3
- weight_out: bfloat16 [1600, 400], replicated, may hold values from -0.15625 to 0.15625
- bias_out: float32 [400], replicated, may hold values from -3 to 3
- layer_scale: float32 [400], P('ch'), may hold values from 0.5 to 2
- cotangent: bfloat16 [400, 64, 4096], P('ch', None, 'lon'), may hold values from -6 to 6
Outputs:
- updated: bfloat16 [400, 64, 4096], P('ch', None, 'lon')
- grad_state: bfloat16 [400, 64, 4096], P('ch', None, 'lon')
- grad_weight_in: float32 [400, 1600], replicated
- grad_weight_out: float32 [1600, 400], replicated
Inputs may be any that keep to these rules, and one draw needn't show every extreme that they name: `sea_mask`: 1 marks an ocean cell, 0 a land cell.
All inputs are finite; a program needn't handle non-finite values. No bound on the sum of `sea_mask` on one device may be relied on, other than what follows from the above.
Results may differ from a plain program's by a relative error of at most 0.0077.
Values may be sent and summed in bfloat16 or wider, within the bound.
No kernel may reach another device: no remote copies, remote signals or barrier semaphores. Data moves between devices by JAX's collectives and lax.ppermute only.
A program may use at most 192 MiB of HBM per device.

v0:
```python
import math
import jax
import jax.numpy as jnp
from jax import lax
from jax.sharding import PartitionSpec as P

KW = 7
root_coef = math.sqrt(2.0 / math.pi)
cubic_coef = 0.044715
norm_eps = 1e-06


def extended(cells, sides, width):
    for axis, dim in sides:
        count = lax.axis_size(axis)
        head = lax.slice_in_dim(cells, 0, width, axis=dim)
        tail = lax.slice_in_dim(cells, cells.shape[dim] - width, cells.shape[dim], axis=dim)
        cells = jnp.concatenate(
            [
                lax.ppermute(tail, axis, [(i, (i + 1) % count) for i in range(count)]),
                cells,
                lax.ppermute(head, axis, [((i + 1) % count, i) for i in range(count)]),
            ],
            axis=dim,
        )
    return cells


def gelu_parts(pre_act):
    inner_arg = root_coef * (pre_act + cubic_coef * pre_act * pre_act * pre_act)
    tangent = jnp.tanh(inner_arg)
    gelu_value = 0.5 * pre_act * (1.0 + tangent)
    gelu_slope = 0.5 * (1.0 + tangent) + 0.5 * pre_act * (1.0 - tangent * tangent) * root_coef * (
        1.0 + 3.0 * cubic_coef * pre_act * pre_act
    )
    return (gelu_value, gelu_slope)


def depth_taps(padded, kernel, row_count, lon_cells):
    tap_total = jnp.zeros((padded.shape[0], row_count, lon_cells), jnp.float32)
    for row_off in range(KW):
        for col_off in range(KW):
            tap_total = (
                tap_total
                + kernel[:, row_off * KW + col_off][:, None, None]
                * padded[:, row_off : row_off + row_count, col_off : col_off + lon_cells]
            )
    return tap_total


def depth_back(padded_grad, kernel, row_count, lon_cells):
    span = KW - 1
    tap_total = jnp.zeros((padded_grad.shape[0], row_count, lon_cells), jnp.float32)
    for row_off in range(KW):
        for col_off in range(KW):
            tap_total = (
                tap_total
                + kernel[:, row_off * KW + col_off][:, None, None]
                * padded_grad[
                    :,
                    span - row_off : span - row_off + row_count,
                    span - col_off : span - col_off + lon_cells,
                ]
            )
    return tap_total


def block_math(
    conv_cells, grad_cells, norm_gain, norm_bias, weight_in, bias_in, weight_out, bias_out
):
    full_width = conv_cells.shape[0]
    values = conv_cells.astype(jnp.float32)
    mean_val = jnp.sum(values, axis=0) / full_width
    square = jnp.sum(values * values, axis=0) / full_width
    inv_std = lax.rsqrt(square - mean_val * mean_val + norm_eps)
    centred = (values - mean_val) * inv_std
    normed = (centred * norm_gain[:, None] + norm_bias[:, None]).astype(jnp.bfloat16)
    pre_act = jnp.dot(weight_in.T, normed, preferred_element_type=jnp.float32) + bias_in[:, None]
    gelu_value, gelu_slope = gelu_parts(pre_act)
    activation = gelu_value.astype(jnp.bfloat16)
    branch = (
        jnp.dot(weight_out.T, activation, preferred_element_type=jnp.float32) + bias_out[:, None]
    ).astype(jnp.bfloat16)
    grad_act = jnp.dot(weight_out, grad_cells, preferred_element_type=jnp.float32)
    grad_pre = (grad_act * gelu_slope).astype(jnp.bfloat16)
    part_out = jnp.dot(activation, grad_cells.T, preferred_element_type=jnp.float32)
    part_in = jnp.dot(normed, grad_pre.T, preferred_element_type=jnp.float32)
    grad_normed = jnp.dot(weight_in, grad_pre, preferred_element_type=jnp.float32)
    scaled_grad = grad_normed * norm_gain[:, None]
    mean_first = jnp.sum(scaled_grad, axis=0) / full_width
    mean_second = jnp.sum(scaled_grad * centred, axis=0) / full_width
    grad_conv = (inv_std * (scaled_grad - mean_first - centred * mean_second)).astype(jnp.bfloat16)
    return (branch, grad_conv, part_in, part_out)


def body(
    ocean_state,
    sea_mask,
    kernel,
    conv_bias,
    norm_gain,
    norm_bias,
    weight_in,
    bias_in,
    weight_out,
    bias_out,
    layer_scale,
    cotangent,
):
    local_chan, row_count, lon_cells = ocean_state.shape
    chan_groups = lax.axis_size("ch")
    full_width = local_chan * chan_groups
    rim_width = KW // 2
    grad_scale = 1.0 / math.sqrt(row_count * lon_cells * lax.axis_size("lon"))
    state_f = ocean_state.astype(jnp.float32)
    state_rim = extended(ocean_state, (("lon", 2),), rim_width)
    padded = jnp.pad(state_rim.astype(jnp.float32), ((0, 0), (rim_width, rim_width), (0, 0)))
    conv_out = (depth_taps(padded, kernel, row_count, lon_cells) + conv_bias[:, None, None]).astype(
        jnp.bfloat16
    )
    mask_f = sea_mask.astype(jnp.float32)[None]
    grad_out = cotangent.astype(jnp.float32) * mask_f
    grad_branch = (grad_out * layer_scale[:, None, None]).astype(jnp.bfloat16)
    quarter = row_count // chan_groups
    conv_cells, grad_cells = (
        lax.all_to_all(conv_out, "ch", split_axis=1, concat_axis=0, tiled=True),
        lax.all_to_all(grad_branch, "ch", split_axis=1, concat_axis=0, tiled=True),
    )
    branch_cells, conv_grad_cells, part_in, part_out = block_math(
        conv_cells.reshape(full_width, quarter * lon_cells),
        grad_cells.reshape(full_width, quarter * lon_cells),
        norm_gain,
        norm_bias,
        weight_in,
        bias_in,
        weight_out,
        bias_out,
    )
    branch, grad_conv = (
        lax.all_to_all(
            branch_cells.reshape(full_width, quarter, lon_cells),
            "ch",
            split_axis=0,
            concat_axis=1,
            tiled=True,
        ),
        lax.all_to_all(
            conv_grad_cells.reshape(full_width, quarter, lon_cells),
            "ch",
            split_axis=0,
            concat_axis=1,
            tiled=True,
        ),
    )
    sum_in, sum_out = lax.psum((part_in, part_out), ("lon", "ch"))
    grad_weight_in = sum_in * grad_scale
    grad_weight_out = sum_out * grad_scale
    updated = (mask_f * (state_f + layer_scale[:, None, None] * branch.astype(jnp.float32))).astype(
        jnp.bfloat16
    )
    grad_rim = extended(grad_conv, (("lon", 2),), rim_width)
    padded_grad = jnp.pad(grad_rim.astype(jnp.float32), ((0, 0), (rim_width, rim_width), (0, 0)))
    grad_state = (grad_out + depth_back(padded_grad, kernel, row_count, lon_cells)).astype(
        jnp.bfloat16
    )
    return (updated, grad_state, grad_weight_in, grad_weight_out)


def solution(mesh):
    return jax.shard_map(
        body,
        mesh=mesh,
        in_specs=(
            P("ch", None, "lon"),
            P(None, "lon"),
            P("ch", None),
            P("ch"),
            P(),
            P(),
            P(),
            P(),
            P(),
            P(),
            P("ch"),
            P("ch", None, "lon"),
        ),
        out_specs=(P("ch", None, "lon"), P("ch", None, "lon"), P(), P()),
        check_vma=False,
    )
```

profile of v0, /device:TPU:1, one launch (start us, length us, event | category | flops | bytes accessed | tf_op | source)
XLA Modules:
  0.0 416.5 jit_solution(18222858004938454714)
XLA Ops:
  7.2 4.5 %fusion.192 = (bf16[100,64,3]{2,1,0:T(8,128)(2,1)}, bf16[100,64,3]{2,1,0:T(8,128)(2,1)}) fusion(bf16[100,64,128]{2,1,0:T(8,128)(2,1)} %param.12), kind=kLoop, calls=%fused_computation.345 | loop fusion | bytes 153600 | tf_op jit(solution)/shard_map/slice | solution.py:17
  19.7 7.5 %collective-permute-start.1 = (bf16[100,64,3]{0,1,2:T(8,128)(2,1)S(1)}, bf16[100,64,3]{0,1,2:T(8,128)(2,1)S(1)}, u32[]{:S(2)}, u32[]{:S(2)}) collective-permute-start(bf16[100,64,3]{0,1,2:T(8,128)(2,1)S(1)} %copy.41), channel_id=1, source_target_pairs={{4,0},{8,4},{12,8},{16,12},{20,16},{24,20},{28,24},{32,28},{36,32}... | collective-permute-start | bytes 115208 | tf_op jit(solution)/shard_map/ppermute | solution.py:22
  33.7 4.3 %maximum_convert_fusion = f32[100,64,134]{2,0,1:T(8,128)S(1)} fusion(bf16[100,64,3]{2,0,1:T(8,128)(2,1)} %copy.28, bf16[100,64,128]{2,0,1:T(8,128)(2,1)} %copy.23, bf16[100,64,3]{2,0,1:T(8,128)(2,1)} %copy.26), kind=kLoop, calls=%fused_computation.82 | loop fusion | flops 5145600 | bytes 5145600 | tf_op jit(solution)/shard_map/convert_element_type | solution.py:117
  38.1 40.2 %add_convert_fusion = bf16[100,64,128]{2,0,1:T(8,128)(2,1)} fusion(f32[100,64,134]{2,0,1:T(8,128)S(1)} %maximum_convert_fusion, f32[100]{0:T(128)} %param.15, f32[100]{0:T(128)} %get-tuple-element.66, f32[100]{0:T(128)} %get-tuple-element.67, f32[100]{0:T(128)S(1)} %get-tuple-element.20, f32[100]{0:T(128)S(1)} %get-tuple-element.21, ...), kind=kLoop, calls=%fused_computation.176 | loop fusion | flops 81100800 | bytes 32333840 | tf_op jit(solution)/shard_map/convert_element_type | solution.py:118
  78.3 25.5 %all_to_all.51 = bf16[100,64,128]{2,0,1:T(8,128)(2,1)S(1)} all-to-all(bf16[100,64,128]{2,0,1:T(8,128)(2,1)} %add_convert_fusion), channel_id=1, replica_groups=mesh['lon'=32,'ch'=4] {'ch'}, dimensions={1} | all-to-all | bytes 3276800 | tf_op jit(solution)/shard_map/all_to_all | solution.py:126
  104.4 10.9 %multiply_convert_fusion = (bf16[1600,2048]{1,0:T(8,128)(2,1)S(1)}, f32[2048,1600]{0,1:T(8,128)}) fusion(f32[1600]{0:T(1024)S(1)} %copy-done.23, bf16[400,1600]{1,0:T(8,128)(2,1)S(1)} %copy-done, f32[50,8,16,128]{3,2,1,0:T(8,128)S(1)} %bitcast.202, f32[400]{0:T(512)S(1)} %copy-done.25, f32[400]{0:T(512)S(1)} %copy-done.26, f32[2048]{0:T(1024)S(1)} %fusion.188, ...), kind=kOutput, calls=%fused_computation.10 | convolution fusion | flops 2658304000 | bytes 24243584 | tf_op jit(solution)/shard_map/dot_general | solution.py:78
  115.3 3.2 fusion.184
  120.2 5.5 %all-to-all-start.1 = ((bf16[400,16,128]{2,1,0:T(8,128)(2,1)}), bf16[400,16,128]{2,1,0:T(8,128)(2,1)}, u32[]{:S(2)}, u32[]{:S(2)}) async-start(bf16[400,16,128]{2,1,0:T(8,128)(2,1)} %bitcast.209), calls=%async_computation.1 | async-start | bytes 3276800 | tf_op jit(solution)/shard_map/all_to_all | solution.py:140
  125.7 20.0 %all-to-all-done.1 = bf16[400,16,128]{2,1,0:T(8,128)(2,1)} async-done(((bf16[400,16,128]{2,1,0:T(8,128)(2,1)}), bf16[400,16,128]{2,1,0:T(8,128)(2,1)}, u32[]{:S(2)}, u32[]{:S(2)}) %all-to-all-start.1) | async-done | bytes 1638432 | tf_op jit(solution)/shard_map/all_to_all | solution.py:140
  147.6 3.6 multiply_convert_fusion.1
  151.2 24.0 %all_to_all.52 = bf16[100,64,128]{2,0,1:T(8,128)(2,1)S(1)} all-to-all(bf16[100,64,128]{2,0,1:T(8,128)(2,1)S(1)} %get-tuple-element.17), channel_id=1, replica_groups=mesh['lon'=32,'ch'=4] {'ch'}, dimensions={1} | all-to-all | bytes 3276800 | tf_op jit(solution)/shard_map/all_to_all | solution.py:127
  175.5 14.4 %fusion.6 = bf16[1600,2048]{1,0:T(8,128)(2,1)S(1)} fusion(f32[2048,1600]{0,1:T(8,128)} %get-tuple-element.69, bf16[1600,400]{0,1:T(8,128)(2,1)S(1)} %copy-done.22, f32[1600]{0:T(1024)S(1)} %copy-done.23, bf16[50,8,16,128]{3,2,1,0:T(8,128)(2,1)S(1)} %bitcast.210), kind=kOutput, calls=%fused_computation.8 | convolution fusion | flops 2686976000 | bytes 22585600 | tf_op jit(solution)/shard_map/dot_general | solution.py:84
  189.9 5.6 %fusion.178 = (f32[2048]{0:T(1024)S(1)}, f32[2048,400]{0,1:T(8,128)}) fusion(f32[50,8,16,128]{3,2,1,0:T(8,128)S(1)} %bitcast.205, f32[2048]{0:T(1024)S(1)} %fusion.188, f32[2048]{0:T(1024)S(1)} %multiply_bitcast_fusion, f32[400]{0:T(512)S(1)} %copy-done.26, bf16[400,1600]{1,0:T(8,128)(2,1)S(1)} %copy-done, bf16[1600,2048]{1,0:T(8,128)(2,1)S(1)} %fusion.6), kind=kOutput, calls=%fused_computation.271 | convolution fusion | flops 2625533952 | bytes 14413376 | tf_op jit(solution)/shard_map/dot_general | solution.py:88
  197.6 4.8 %fusion.180 = bf16[50,8,16,128]{3,1,2,0:T(8,128)(2,1)S(1)} fusion(f32[50,8,16,128]{3,2,1,0:T(8,128)} %bitcast.203, f32[2048,400]{0,1:T(8,128)} %get-tuple-element.71, f32[2048]{0:T(1024)S(1)} %get-tuple-element.72, f32[2048]{0:T(1024)S(1)} %get-tuple-element.73, f32[2048]{0:T(1024)S(1)} %fusion.188, f32[2048]{0:T(1024)S(1)} %multiply_bitcast_fusion), kind=kLoop, calls=%fused_computation.278 | loop fusion | flops 5734400 | bytes 8224768
  204.0 5.4 %all-to-all-start.3 = ((bf16[400,16,128]{2,1,0:T(8,128)(2,1)}), bf16[400,16,128]{2,1,0:T(8,128)(2,1)}, u32[]{:S(2)}, u32[]{:S(2)}) async-start(bf16[400,16,128]{2,1,0:T(8,128)(2,1)} %bitcast.208), calls=%async_computation.3 | async-start | bytes 3276800 | tf_op jit(solution)/shard_map/all_to_all | solution.py:147
  211.2 9.2 %fusion.189 = f32[400,1600]{1,0:T(8,128)} fusion(bf16[1600,2048]{1,0:T(8,128)(2,1)} %copy-done.27, f32[50,8,16,128]{3,2,1,0:T(8,128)} %bitcast.204, f32[400]{0:T(512)S(1)} %copy-done.25, f32[400]{0:T(512)S(1)} %copy-done.26, f32[2048]{0:T(1024)S(1)} %fusion.188, f32[2048]{0:T(1024)S(1)} %multiply_bitcast_fusion), kind=kOutput, calls=%fused_computation.342 | convolution fusion | flops 2625536000 | bytes 12409984 | tf_op jit(solution)/shard_map/dot_general | solution.py:87
  220.4 9.0 %all-to-all-done.3 = bf16[400,16,128]{2,1,0:T(8,128)(2,1)} async-done(((bf16[400,16,128]{2,1,0:T(8,128)(2,1)}), bf16[400,16,128]{2,1,0:T(8,128)(2,1)}, u32[]{:S(2)}, u32[]{:S(2)}) %all-to-all-start.3) | async-done | bytes 1638432 | tf_op jit(solution)/shard_map/all_to_all | solution.py:147
  236.0 7.5 %collective-permute-start.3 = (bf16[100,64,3]{0,1,2:T(8,128)(2,1)S(1)}, bf16[100,64,3]{0,1,2:T(8,128)(2,1)S(1)}, u32[]{:S(2)}, u32[]{:S(2)}) collective-permute-start(bf16[100,64,3]{0,1,2:T(8,128)(2,1)S(1)} %copy.35), channel_id=1, source_target_pairs={{4,0},{8,4},{12,8},{16,12},{20,16},{24,20},{28,24},{32,28},{36,32}... | collective-permute-start | bytes 115208 | tf_op jit(solution)/shard_map/ppermute | solution.py:22
  243.5 8.0 %fusion.181 = f32[1600,400]{0,1:T(8,128)} fusion(bf16[1600,2048]{1,0:T(8,128)(2,1)} %copy-done.28, bf16[50,8,16,128]{3,2,1,0:T(8,128)(2,1)} %bitcast.211), kind=kOutput, calls=%fused_computation.279 | convolution fusion | flops 2621440000 | bytes 10752000 | tf_op jit(solution)/shard_map/dot_general | solution.py:86
  255.2 4.7 %maximum_convert_fusion.1 = f32[100,64,134]{2,0,1:T(8,128)S(1)} fusion(bf16[100,64,3]{2,0,1:T(8,128)(2,1)} %copy.37, bf16[100,64,128]{2,0,1:T(8,128)(2,1)} %bitcast.201, bf16[100,64,3]{2,0,1:T(8,128)(2,1)} %copy.36), kind=kLoop, calls=%fused_computation.83 | loop fusion | flops 5145600 | bytes 5145600 | tf_op jit(solution)/shard_map/convert_element_type | solution.py:162
  259.9 41.0 %fusion.173 = bf16[100,64,128]{2,0,1:T(8,128)(2,1)} fusion(f32[100,64,134]{2,0,1:T(8,128)S(1)} %maximum_convert_fusion.1, f32[100]{0:T(128)} %get-tuple-element.66, f32[100]{0:T(128)} %get-tuple-element.67, f32[100]{0:T(128)S(1)} %get-tuple-element.20, f32[100]{0:T(128)S(1)} %get-tuple-element.21, f32[100]{0:T(128)S(1)} %get-tuple-element.22, ...), kind=kLoop, calls=%fused_computation.263 | loop fusion | flops 82739200 | bytes 34003712 | tf_op jit(solution)/shard_map/convert_element_type | solution.py:163
  300.9 3.1 copy.39
  304.0 100.2 %all-reduce.5.cloned.1.call-done = (f32[400,1600]{1,0:T(8,128)}, f32[1600,400]{0,1:T(8,128)}) async-done(((f32[400,1600]{1,0:T(8,128)}, f32[1600,400]{0,1:T(8,128)}), (f32[400,1600]{1,0:T(8,128)}, f32[1600,400]{0,1:T(8,128)})) %all-reduce.5.cloned.1.call-update) | async-done | bytes 5120016 | tf_op jit(solution)/shard_map/psum | solution.py:155
  404.2 3.6 broadcast_multiply_fusion
  (92 shorter events, 36.3 us)
Async XLA Ops:
  7.2 97.1 %copy-start = (bf16[400,1600]{1,0:T(8,128)(2,1)S(1)}, bf16[400,1600]{1,0:T(8,128)(2,1)}, u32[]{:S(2)}) copy-start(bf16[400,1600]{1,0:T(8,128)(2,1)} %param.18) | copy-start | bytes 3840004
  7.2 20.6 %copy-start.2 = (bf16[100,64,128]{2,1,0:T(8,128)(2,1)S(1)}, bf16[100,64,128]{2,1,0:T(8,128)(2,1)}, u32[]{:S(2)}) copy-start(bf16[100,64,128]{2,1,0:T(8,128)(2,1)} %param.12) | copy-start | bytes 4915204
  7.2 19.9 %copy-start.11 = (f32[100,49]{0,1:T(8,128)S(1)}, f32[100,49]{0,1:T(8,128)}, u32[]{:S(2)}) copy-start(f32[100,49]{0,1:T(8,128)} %param.14) | copy-start | bytes 58804
  14.6 15.5 %collective-permute-start = (bf16[100,64,3]{0,1,2:T(8,128)(2,1)S(1)}, bf16[100,64,3]{0,1,2:T(8,128)(2,1)S(1)}, u32[]{:S(2)}, u32[]{:S(2)}) collective-permute-start(bf16[100,64,3]{0,1,2:T(8,128)(2,1)S(1)} %copy.40), channel_id=1, source_target_pairs={{0,4},{4,8},{8,12},{12,16},{16,20},{20,24},{24,28},{28,32},{32,36}... | collective-permute-start | bytes 115208 | tf_op jit(solution)/shard_map/ppermute | solution.py:20
  19.7 12.2 %collective-permute-start.1 = (bf16[100,64,3]{0,1,2:T(8,128)(2,1)S(1)}, bf16[100,64,3]{0,1,2:T(8,128)(2,1)S(1)}, u32[]{:S(2)}, u32[]{:S(2)}) collective-permute-start(bf16[100,64,3]{0,1,2:T(8,128)(2,1)S(1)} %copy.41), channel_id=1, source_target_pairs={{4,0},{8,4},{12,8},{16,12},{20,16},{24,20},{28,24},{32,28},{36,32}... | collective-permute-start | bytes 115208 | tf_op jit(solution)/shard_map/ppermute | solution.py:22
  27.2 10.8 %copy-start.12 = (f32[100]{0:T(128)}, f32[100]{0:T(128)S(1)}, u32[]{:S(2)}) copy-start(f32[100]{0:T(128)S(1)} %get-tuple-element.52) | copy-start | bytes 1204
  27.2 10.8 %copy-start.13 = (f32[100]{0:T(128)}, f32[100]{0:T(128)S(1)}, u32[]{:S(2)}) copy-start(f32[100]{0:T(128)S(1)} %get-tuple-element.53) | copy-start | bytes 1204
  27.2 10.8 %copy-start.14 = (f32[100]{0:T(128)}, f32[100]{0:T(128)S(1)}, u32[]{:S(2)}) copy-start(f32[100]{0:T(128)S(1)} %get-tuple-element.54) | copy-start | bytes 1204
  78.2 26.1 %copy-start.23 = (f32[1600]{0:T(1024)S(1)}, f32[1600]{0:T(1024)}, u32[]{:S(2)}) copy-start(f32[1600]{0:T(1024)} %param.19) | copy-start | bytes 19204
  78.2 26.1 %copy-start.25 = (f32[400]{0:T(512)S(1)}, f32[400]{0:T(512)}, u32[]{:S(2)}) copy-start(f32[400]{0:T(512)} %param.17) | copy-start | bytes 4804
  78.3 26.1 %copy-start.26 = (f32[400]{0:T(512)S(1)}, f32[400]{0:T(512)}, u32[]{:S(2)}) copy-start(f32[400]{0:T(512)} %param.16) | copy-start | bytes 4804
  104.3 11.0 %copy-start.4 = (f32[100,4,16,128]{3,2,0,1:T(8,128)}, f32[100,4,16,128]{3,2,0,1:T(8,128)S(1)}, u32[]{:S(2)}) copy-start(f32[100,4,16,128]{3,2,0,1:T(8,128)S(1)} %get-tuple-element.12) | copy-start | bytes 9830404
  104.3 11.0 %copy-start.21 = (bf16[1600,400]{0,1:T(8,128)(2,1)S(1)}, bf16[1600,400]{0,1:T(8,128)(2,1)}, u32[]{:S(2)}) copy-start(bf16[1600,400]{0,1:T(8,128)(2,1)} %param.20) | copy-start | bytes 3840004
  104.3 11.0 %copy-start.24 = (f32[400]{0:T(512)S(1)}, f32[400]{0:T(512)}, u32[]{:S(2)}) copy-start(f32[400]{0:T(512)} %param.21) | copy-start | bytes 4804
  120.2 27.4 %copy-start.3 = (bf16[100,64,128]{2,1,0:T(8,128)(2,1)S(1)}, bf16[100,64,128]{2,1,0:T(8,128)(2,1)}, u32[]{:S(2)}) copy-start(bf16[100,64,128]{2,1,0:T(8,128)(2,1)} %param.12) | copy-start | bytes 4915204
  120.2 27.4 %copy-start.20 = (f32[100]{0:T(128)S(1)}, f32[100]{0:T(128)}, u32[]{:S(2)}) copy-start(f32[100]{0:T(128)} %param.22) | copy-start | bytes 1204
  120.2 25.5 %all-to-all-start.1 = ((bf16[400,16,128]{2,1,0:T(8,128)(2,1)}), bf16[400,16,128]{2,1,0:T(8,128)(2,1)}, u32[]{:S(2)}, u32[]{:S(2)}) async-start(bf16[400,16,128]{2,1,0:T(8,128)(2,1)} %bitcast.209), calls=%async_computation.1 | async-start | bytes 3276800 | tf_op jit(solution)/shard_map/all_to_all | solution.py:140
  151.2 24.3 %copy-start.22 = (bf16[1600,400]{0,1:T(8,128)(2,1)S(1)}, bf16[1600,400]{0,1:T(8,128)(2,1)}, u32[]{:S(2)}) copy-start(bf16[1600,400]{0,1:T(8,128)(2,1)} %param.20) | copy-start | bytes 3840004
  175.5 14.4 %copy-start.9 = (bf16[100,4,16,128]{3,2,0,1:T(8,128)(2,1)}, bf16[100,4,16,128]{3,2,0,1:T(8,128)(2,1)S(1)}, u32[]{:S(2)}) copy-start(bf16[100,4,16,128]{3,2,0,1:T(8,128)(2,1)S(1)} %copy.32) | copy-start | bytes 4915204
  175.5 14.4 %copy-start.5 = (f32[100,4,16,128]{3,2,0,1:T(8,128)S(1)}, f32[100,4,16,128]{3,2,0,1:T(8,128)}, u32[]{:S(2)}) copy-start(f32[100,4,16,128]{3,2,0,1:T(8,128)} %copy-done.4) | copy-start | bytes 9830404
  204.0 25.4 %all-to-all-start.3 = ((bf16[400,16,128]{2,1,0:T(8,128)(2,1)}), bf16[400,16,128]{2,1,0:T(8,128)(2,1)}, u32[]{:S(2)}, u32[]{:S(2)}) async-start(bf16[400,16,128]{2,1,0:T(8,128)(2,1)} %bitcast.208), calls=%async_computation.3 | async-start | bytes 3276800 | tf_op jit(solution)/shard_map/all_to_all | solution.py:147
  209.4 194.8 %all-reduce.5.cloned.1.call-start = ((), (), s32[]{:S(2)}) async-start(), calls=%async_computation.4 | async-start | bytes 10649600 | tf_op jit(solution)/shard_map/psum | solution.py:155
  235.0 16.5 %collective-permute-start.2 = (bf16[100,64,3]{0,1,2:T(8,128)(2,1)S(1)}, bf16[100,64,3]{0,1,2:T(8,128)(2,1)S(1)}, u32[]{:S(2)}, u32[]{:S(2)}) collective-permute-start(bf16[100,64,3]{0,1,2:T(8,128)(2,1)S(1)} %copy.34), channel_id=1, source_target_pairs={{0,4},{4,8},{8,12},{12,16},{16,20},{20,24},{24,28},{28,32},{32,36}... | collective-permute-start | bytes 115208 | tf_op jit(solution)/shard_map/ppermute | solution.py:20
  236.0 17.3 %collective-permute-start.3 = (bf16[100,64,3]{0,1,2:T(8,128)(2,1)S(1)}, bf16[100,64,3]{0,1,2:T(8,128)(2,1)S(1)}, u32[]{:S(2)}, u32[]{:S(2)}) collective-permute-start(bf16[100,64,3]{0,1,2:T(8,128)(2,1)S(1)} %copy.35), channel_id=1, source_target_pairs={{4,0},{8,4},{12,8},{16,12},{20,16},{24,20},{28,24},{32,28},{36,32}... | collective-permute-start | bytes 115208 | tf_op jit(solution)/shard_map/ppermute | solution.py:22
  (12 other events, 82.7 us)
Sparse Core Ops, SparseCore 0:
  251.6 152.4 all-reduce.4
where the time goes:
time: 424 us; the launch traced here: 417 us
  waiting for transfers between devices  129 us (30%)
  other arithmetic  106 us (25%)
  matrix products  51.3 us (12%)
  blocking collectives  49.6 us (12%)
  local copies, waits for them, and re-layouts  37 us (9%)
  starting transfers between devices  28.3 us (7%)
  between operations  14.7 us (3%)
    psum x1, waiting for transfers between devices, body(): sum_in, sum_out = lax.psum((part_in, part_out), ('lon', 'ch'))  100 us
    convert_element_type x1, other arithmetic, body(): (grad_out + depth_back(padded_grad, kernel, row_count, lon_cells)).astype...  41 us
    convert_element_type x1, other arithmetic, body(): (depth_taps(padded, kernel, row_count, lon_cells) + conv_bias[:, None, No...  40.2 us
    all_to_all x1, blocking collectives, body(): lax.all_to_all(conv_out, 'ch', split_axis=1, concat_axis=0, tiled=True)  25.5 us
    all_to_all x1, blocking collectives, body(): lax.all_to_all(grad_branch, 'ch', split_axis=1, concat_axis=0, tiled=True)  24 us
    all_to_all x1, waiting for transfers between devices, body(): lax.all_to_all(branch_cells.reshape(full_width, quarter, lon_cells), 'ch'...  20 us
    unnamed x65, local copies, waits for them, and re-layouts  16.1 us
    ppermute x2, starting transfers between devices, extended(): lax.ppermute(head, axis, [((i + 1) % count, i) for i in range(count)])  15 us
  transfers between devices with their start and end apart: 7, of which 3 were waited for; matrix products, arithmetic and copies ran while one was open for 19% of the time, Pallas kernels for 0%

commit v1 on v0

--- a/solution.py
+++ b/solution.py
@@ -152,7 +152,11 @@
             tiled=True,
         ),
     )
-    sum_in, sum_out = lax.psum((part_in, part_out), ("lon", "ch"))
+
+    def deliver_trails(row_axis, across, xx):
+        return jax.lax.psum(jax.lax.psum(xx, row_axis), across)
+
+    sum_in, sum_out = deliver_trails("ch", "lon", (part_in, part_out))
     grad_weight_in = sum_in * grad_scale
     grad_weight_out = sum_out * grad_scale
     updated = (mask_f * (state_f + layer_scale[:, None, None] * branch.astype(jnp.float32))).astype(

time: 424 us -> 724 us (1.71)
  the two profiles are of different devices: /device:TPU:1 before, /device:TPU:0 now
where the time goes in v1:
time: 724 us; the launch traced here: 717 us
  waiting for transfers between devices  433 us (60%)
  other arithmetic  106 us (15%)
  blocking collectives  49.7 us (7%)
  matrix products  47.5 us (7%)
  local copies, waits for them, and re-layouts  40 us (6%)
  starting transfers between devices  25.2 us (3%)
  between operations  14.8 us (2%)
    psum x2, waiting for transfers between devices, deliver_trails(): return jax.lax.psum(jax.lax.psum(xx, row_axis), across)  412 us
    convert_element_type x1, other arithmetic, body(): (grad_out + depth_back(padded_grad, kernel, row_count, lon_cells)).astype...  41 us
    convert_element_type x1, other arithmetic, body(): (depth_taps(padded, kernel, row_count, lon_cells) + conv_bias[:, None, No...  40.2 us
    all_to_all x1, blocking collectives, body(): lax.all_to_all(conv_out, 'ch', split_axis=1, concat_axis=0, tiled=True)  25.6 us
    all_to_all x1, blocking collectives, body(): lax.all_to_all(grad_branch, 'ch', split_axis=1, concat_axis=0, tiled=True)  24.1 us
    all_to_all x1, waiting for transfers between devices, body(): lax.all_to_all(branch_cells.reshape(full_width, quarter, lon_cells), 'ch'...  20.8 us
    unnamed x67, local copies, waits for them, and re-layouts  18.8 us
  transfers between devices with their start and end apart: 8, of which 3 were waited for; matrix products, arithmetic and copies ran while one was open for 12% of the time, Pallas kernels for 0%

profile of v1, /device:TPU:0, one launch (start us, length us, event | category | flops | bytes accessed | tf_op | source)
XLA Modules:
  0.0 716.6 jit_solution(470799908180663181)
XLA Ops:
  7.2 4.5 fusion.192
  19.2 7.5 %collective-permute-start.1 = (bf16[100,64,3]{0,1,2:T(8,128)(2,1)S(1)}, bf16[100,64,3]{0,1,2:T(8,128)(2,1)S(1)}, u32[]{:S(2)}, u32[]{:S(2)}) collective-permute-start(bf16[100,64,3]{0,1,2:T(8,128)(2,1)S(1)} %copy.41), channel_id=1, source_target_pairs={{4,0},{8,4},{12,8},{16,12},{20,16},{24,20},{28,24},{32,28},{36,32}... | collective-permute-start | bytes 115208 | tf_op jit(solution)/shard_map/ppermute | solution.py:22
  33.2 4.3 maximum_convert_fusion
  37.6 40.2 %add_convert_fusion = bf16[100,64,128]{2,0,1:T(8,128)(2,1)} fusion(f32[100,64,134]{2,0,1:T(8,128)S(1)} %maximum_convert_fusion, f32[100]{0:T(128)} %param.15, f32[100]{0:T(128)} %get-tuple-element.68, f32[100]{0:T(128)} %get-tuple-element.69, f32[100]{0:T(128)S(1)} %get-tuple-element.22, f32[100]{0:T(128)S(1)} %get-tuple-element.23, ...), kind=kLoop, calls=%fused_computation.176 | loop fusion | flops 81100800 | bytes 32333840 | tf_op jit(solution)/shard_map/convert_element_type | solution.py:118
  77.8 25.6 %all_to_all.51 = bf16[100,64,128]{2,0,1:T(8,128)(2,1)S(1)} all-to-all(bf16[100,64,128]{2,0,1:T(8,128)(2,1)} %add_convert_fusion), channel_id=1, replica_groups=mesh['lon'=32,'ch'=4] {'ch'}, dimensions={1} | all-to-all | bytes 3276800 | tf_op jit(solution)/shard_map/all_to_all | solution.py:126
  104.0 11.0 %multiply_convert_fusion = (bf16[1600,2048]{1,0:T(8,128)(2,1)S(1)}, f32[2048,1600]{0,1:T(8,128)}) fusion(f32[1600]{0:T(1024)S(1)} %copy-done.22, bf16[400,1600]{1,0:T(8,128)(2,1)S(1)} %copy-done, f32[50,8,16,128]{3,2,1,0:T(8,128)S(1)} %bitcast.202, f32[400]{0:T(512)S(1)} %copy-done.24, f32[400]{0:T(512)S(1)} %copy-done.25, f32[2048]{0:T(1024)S(1)} %fusion.188, ...), kind=kOutput, calls=%fused_computation.10 | convolution fusion | flops 2658304000 | bytes 24243584 | tf_op jit(solution)/shard_map/dot_general | solution.py:78
  115.0 3.2 fusion.184
  119.9 4.5 all-to-all-start.1
  124.5 20.8 %all-to-all-done.1 = bf16[400,16,128]{2,1,0:T(8,128)(2,1)} async-done(((bf16[400,16,128]{2,1,0:T(8,128)(2,1)}), bf16[400,16,128]{2,1,0:T(8,128)(2,1)}, u32[]{:S(2)}, u32[]{:S(2)}) %all-to-all-start.1) | async-done | bytes 1638432 | tf_op jit(solution)/shard_map/all_to_all | solution.py:140
  147.2 3.6 multiply_convert_fusion.1
  150.8 24.1 %all_to_all.52 = bf16[100,64,128]{2,0,1:T(8,128)(2,1)S(1)} all-to-all(bf16[100,64,128]{2,0,1:T(8,128)(2,1)S(1)} %get-tuple-element.19), channel_id=1, replica_groups=mesh['lon'=32,'ch'=4] {'ch'}, dimensions={1} | all-to-all | bytes 3276800 | tf_op jit(solution)/shard_map/all_to_all | solution.py:127
  175.2 4.7 fusion.181
  179.9 13.9 %fusion.6 = bf16[1600,2048]{1,0:T(8,128)(2,1)S(1)} fusion(f32[2048,1600]{0,1:T(8,128)} %get-tuple-element.71, bf16[1600,400]{0,1:T(8,128)(2,1)S(1)} %copy-done.21, f32[1600]{0:T(1024)S(1)} %copy-done.22, bf16[50,8,16,128]{3,2,1,0:T(8,128)(2,1)S(1)} %bitcast.212), kind=kOutput, calls=%fused_computation.8 | convolution fusion | flops 2686976000 | bytes 22585600 | tf_op jit(solution)/shard_map/dot_general | solution.py:84
  196.5 5.5 fusion.189
  202.1 9.2 %fusion.178 = (f32[2048]{0:T(1024)S(1)}, f32[2048,400]{0,1:T(8,128)}) fusion(f32[50,8,16,128]{3,2,1,0:T(8,128)} %bitcast.203, f32[2048]{0:T(1024)S(1)} %fusion.188, f32[2048]{0:T(1024)S(1)} %multiply_bitcast_fusion, f32[400]{0:T(512)S(1)} %copy-done.25, bf16[400,1600]{1,0:T(8,128)(2,1)S(1)} %copy-done, bf16[1600,2048]{1,0:T(8,128)(2,1)} %copy-done.26), kind=kOutput, calls=%fused_computation.271 | convolution fusion | flops 2625533952 | bytes 14413376 | tf_op jit(solution)/shard_map/dot_general | solution.py:88
  213.4 4.8 fusion.180
  219.8 3.6 all-to-all-start.3
  223.5 104.6 %all-reduce.9.cloned.1.call-done = (f32[400,1600]{1,0:T(8,128)}, f32[1600,400]{0,1:T(8,128)}) async-done(((f32[400,1600]{1,0:T(8,128)}, f32[1600,400]{0,1:T(8,128)}), (f32[400,1600]{1,0:T(8,128)}, f32[1600,400]{0,1:T(8,128)})) %all-reduce.9.cloned.1.call-update) | async-done | bytes 5120016 | tf_op jit(solution)/shard_map/psum | solution.py:157
  336.4 6.3 collective-permute-start.3
  348.0 4.3 maximum_convert_fusion.1
  352.3 41.0 %fusion.173 = bf16[100,64,128]{2,0,1:T(8,128)(2,1)} fusion(f32[100,64,134]{2,0,1:T(8,128)S(1)} %maximum_convert_fusion.1, f32[100]{0:T(128)} %get-tuple-element.68, f32[100]{0:T(128)} %get-tuple-element.69, f32[100]{0:T(128)S(1)} %get-tuple-element.22, f32[100]{0:T(128)S(1)} %get-tuple-element.23, f32[100]{0:T(128)S(1)} %get-tuple-element.24, ...), kind=kLoop, calls=%fused_computation.263 | loop fusion | flops 82739200 | bytes 34003712 | tf_op jit(solution)/shard_map/convert_element_type | solution.py:167
  393.3 3.1 copy.39
  396.3 307.9 %all-reduce.7.cloned.1.call-done = (f32[400,1600]{1,0:T(8,128)}, f32[1600,400]{0,1:T(8,128)}) async-done(((f32[400,1600]{1,0:T(8,128)}, f32[1600,400]{0,1:T(8,128)}), (f32[400,1600]{1,0:T(8,128)}, f32[1600,400]{0,1:T(8,128)})) %all-reduce.7.cloned.1.call-update) | async-done | bytes 5120016 | tf_op jit(solution)/shard_map/psum | solution.py:157
  704.2 3.6 broadcast_multiply_fusion
  (98 shorter events, 40.1 us)
Async XLA Ops:
  7.2 96.8 %copy-start = (bf16[400,1600]{1,0:T(8,128)(2,1)S(1)}, bf16[400,1600]{1,0:T(8,128)(2,1)}, u32[]{:S(2)}) copy-start(bf16[400,1600]{1,0:T(8,128)(2,1)} %param.18) | copy-start | bytes 3840004
  7.2 20.2 %copy-start.2 = (bf16[100,64,128]{2,1,0:T(8,128)(2,1)S(1)}, bf16[100,64,128]{2,1,0:T(8,128)(2,1)}, u32[]{:S(2)}) copy-start(bf16[100,64,128]{2,1,0:T(8,128)(2,1)} %param.12) | copy-start | bytes 4915204
  7.2 19.5 %copy-start.10 = (f32[100,49]{0,1:T(8,128)S(1)}, f32[100,49]{0,1:T(8,128)}, u32[]{:S(2)}) copy-start(f32[100,49]{0,1:T(8,128)} %param.14) | copy-start | bytes 58804
  14.6 15.1 %collective-permute-start = (bf16[100,64,3]{0,1,2:T(8,128)(2,1)S(1)}, bf16[100,64,3]{0,1,2:T(8,128)(2,1)S(1)}, u32[]{:S(2)}, u32[]{:S(2)}) collective-permute-start(bf16[100,64,3]{0,1,2:T(8,128)(2,1)S(1)} %copy.40), channel_id=1, source_target_pairs={{0,4},{4,8},{8,12},{12,16},{16,20},{20,24},{24,28},{28,32},{32,36}... | collective-permute-start | bytes 115208 | tf_op jit(solution)/shard_map/ppermute | solution.py:20
  19.2 12.3 %collective-permute-start.1 = (bf16[100,64,3]{0,1,2:T(8,128)(2,1)S(1)}, bf16[100,64,3]{0,1,2:T(8,128)(2,1)S(1)}, u32[]{:S(2)}, u32[]{:S(2)}) collective-permute-start(bf16[100,64,3]{0,1,2:T(8,128)(2,1)S(1)} %copy.41), channel_id=1, source_target_pairs={{4,0},{8,4},{12,8},{16,12},{20,16},{24,20},{28,24},{32,28},{36,32}... | collective-permute-start | bytes 115208 | tf_op jit(solution)/shard_map/ppermute | solution.py:22
  26.7 10.8 %copy-start.11 = (f32[100]{0:T(128)}, f32[100]{0:T(128)S(1)}, u32[]{:S(2)}) copy-start(f32[100]{0:T(128)S(1)} %get-tuple-element.54) | copy-start | bytes 1204
  77.8 26.2 %copy-start.22 = (f32[1600]{0:T(1024)S(1)}, f32[1600]{0:T(1024)}, u32[]{:S(2)}) copy-start(f32[1600]{0:T(1024)} %param.19) | copy-start | bytes 19204
  77.8 26.2 %copy-start.24 = (f32[400]{0:T(512)S(1)}, f32[400]{0:T(512)}, u32[]{:S(2)}) copy-start(f32[400]{0:T(512)} %param.17) | copy-start | bytes 4804
  77.8 26.2 %copy-start.25 = (f32[400]{0:T(512)S(1)}, f32[400]{0:T(512)}, u32[]{:S(2)}) copy-start(f32[400]{0:T(512)} %param.16) | copy-start | bytes 4804
  103.9 11.1 %copy-start.4 = (f32[100,4,16,128]{3,2,0,1:T(8,128)}, f32[100,4,16,128]{3,2,0,1:T(8,128)S(1)}, u32[]{:S(2)}) copy-start(f32[100,4,16,128]{3,2,0,1:T(8,128)S(1)} %get-tuple-element.14) | copy-start | bytes 9830404
  104.0 11.0 %copy-start.20 = (bf16[1600,400]{0,1:T(8,128)(2,1)S(1)}, bf16[1600,400]{0,1:T(8,128)(2,1)}, u32[]{:S(2)}) copy-start(bf16[1600,400]{0,1:T(8,128)(2,1)} %param.20) | copy-start | bytes 3840004
  104.0 11.0 %copy-start.23 = (f32[400]{0:T(512)S(1)}, f32[400]{0:T(512)}, u32[]{:S(2)}) copy-start(f32[400]{0:T(512)} %param.21) | copy-start | bytes 4804
  119.9 27.3 %copy-start.3 = (bf16[100,64,128]{2,1,0:T(8,128)(2,1)S(1)}, bf16[100,64,128]{2,1,0:T(8,128)(2,1)}, u32[]{:S(2)}) copy-start(bf16[100,64,128]{2,1,0:T(8,128)(2,1)} %param.12) | copy-start | bytes 4915204
  119.9 27.3 %copy-start.19 = (f32[100]{0:T(128)S(1)}, f32[100]{0:T(128)}, u32[]{:S(2)}) copy-start(f32[100]{0:T(128)} %param.22) | copy-start | bytes 1204
  119.9 25.4 %all-to-all-start.1 = ((bf16[400,16,128]{2,1,0:T(8,128)(2,1)}), bf16[400,16,128]{2,1,0:T(8,128)(2,1)}, u32[]{:S(2)}, u32[]{:S(2)}) async-start(bf16[400,16,128]{2,1,0:T(8,128)(2,1)} %bitcast.210), calls=%async_computation.1 | async-start | bytes 3276800 | tf_op jit(solution)/shard_map/all_to_all | solution.py:140
  124.4 203.6 %all-reduce.9.cloned.1.call-start = ((), (), s32[]{:S(2)}) async-start(), calls=%async_computation.5 | async-start | bytes 10649600 | tf_op jit(solution)/shard_map/psum | solution.py:157
  145.3 29.9 %slice-start = ((s8[6553600]{0:T(1024)(128)(4,1)}), s8[4194304]{0:T(1024)(128)(4,1)S(1)}, s32[]{:S(2)}) async-start(s8[6553600]{0:T(1024)(128)(4,1)} %bitcast.213), calls=%async_computation.6 | async-start | bytes 8388608
  147.2 28.0 %slice-start.1 = ((s8[6553600]{0:T(1024)(128)(4,1)}), s8[2359296]{0:T(1024)(128)(4,1)S(1)}, s32[]{:S(2)}) async-start(s8[6553600]{0:T(1024)(128)(4,1)} %bitcast.213), calls=%async_computation.7 | async-start | bytes 4718592
  179.9 16.7 %copy-start.5 = (f32[100,4,16,128]{3,2,0,1:T(8,128)S(1)}, f32[100,4,16,128]{3,2,0,1:T(8,128)}, u32[]{:S(2)}) copy-start(f32[100,4,16,128]{3,2,0,1:T(8,128)} %copy-done.4) | copy-start | bytes 9830404
  219.8 108.3 %all-to-all-start.3 = ((bf16[400,16,128]{2,1,0:T(8,128)(2,1)}), bf16[400,16,128]{2,1,0:T(8,128)(2,1)S(1)}, u32[]{:S(2)}, u32[]{:S(2)}) async-start(bf16[400,16,128]{2,1,0:T(8,128)(2,1)} %bitcast.209), calls=%async_computation.3 | async-start | bytes 3276800 | tf_op jit(solution)/shard_map/all_to_all | solution.py:147
  223.4 480.8 %all-reduce.7.cloned.1.call-start = ((), (), s32[]{:S(2)}) async-start(), calls=%async_computation.4 | async-start | bytes 10649600 | tf_op jit(solution)/shard_map/psum | solution.py:157
  330.9 11.9 %copy-start.6 = (bf16[100,64,128]{2,0,1:T(8,128)(2,1)S(1)}, bf16[100,64,128]{2,0,1:T(8,128)(2,1)}, u32[]{:S(2)}) copy-start(bf16[100,64,128]{2,0,1:T(8,128)(2,1)} %get-tuple-element.20) | copy-start | bytes 4915204
  333.0 11.4 %collective-permute-start.2 = (bf16[100,64,3]{0,1,2:T(8,128)(2,1)S(1)}, bf16[100,64,3]{0,1,2:T(8,128)(2,1)S(1)}, u32[]{:S(2)}, u32[]{:S(2)}) collective-permute-start(bf16[100,64,3]{0,1,2:T(8,128)(2,1)S(1)} %copy.34), channel_id=1, source_target_pairs={{0,4},{4,8},{8,12},{12,16},{16,20},{20,24},{24,28},{28,32},{32,36}... | collective-permute-start | bytes 115208 | tf_op jit(solution)/shard_map/ppermute | solution.py:20
  336.4 9.7 %collective-permute-start.3 = (bf16[100,64,3]{0,1,2:T(8,128)(2,1)S(1)}, bf16[100,64,3]{0,1,2:T(8,128)(2,1)S(1)}, u32[]{:S(2)}, u32[]{:S(2)}) collective-permute-start(bf16[100,64,3]{0,1,2:T(8,128)(2,1)S(1)} %copy.35), channel_id=1, source_target_pairs={{4,0},{8,4},{12,8},{16,12},{20,16},{24,20},{28,24},{32,28},{36,32}... | collective-permute-start | bytes 115208 | tf_op jit(solution)/shard_map/ppermute | solution.py:22
  (14 other events, 98.8 us)
Sparse Core Ops, SparseCore 0:
  202.2 125.8 all-reduce.8
  330.7 373.5 all-reduce.6
